TPU v7x, 256 devices: a whole 4x4x8 slice. The times are simulated.
256 devices in a mesh: row: 16 (over y, x), col: 16 (over z, core).
Axes of the slice: x: 4, y: 4, z: 8, core: 2. Of those that a mesh axis runs over, the one named last changes fastest.
Arguments:
- factor_diag: float32 [2, 512, 512], replicated, as said below
- factor_mid: float32 [512, 512], replicated, may hold values from -0.25 to 0.25
- factor_low: float32 [2, 16384, 512], P(None, ('row', 'col')), may hold values from -0.046875 to 0.046875
- adjoint_diag: float32 [2, 512, 512], replicated, may hold values from -6 to 6
- adjoint_mid: float32 [512, 512], replicated, may hold values from -6 to 6
- adjoint_low: float32 [2, 16384, 512], P(None, ('row', 'col')), may hold values from -6 to 6
- trailing_adjoint: float32 [16384, 16, 1024], P('row', None, 'col'), as said below
Outputs:
- grad_diag: float32 [2, 512, 512], replicated
- grad_mid: float32 [512, 512], replicated
- grad_low: float32 [2, 16384, 512], P(None, ('row', 'col'))
Inputs may be any that keep to these rules, and one draw needn't show every extreme that they name: `factor_diag`: each of the two [512, 512] blocks is lower triangular with diagonal entries between 1 and 2. `trailing_adjoint`: symmetric when read as an 16384 x 16384 matrix in row-major order.
All inputs are finite; a program needn't handle non-finite values.
Results may differ from a plain program's by a relative error of at most 0.000065.
Values sent between devices are 32-bit elements; how exact they have to be, the bound alone decides.
No kernel may reach another device: no remote copies, remote signals or barrier semaphores. Data moves between devices by JAX's collectives and lax.ppermute only.
A program may use at most 128 MiB of HBM per device.

v0:
```python
import jax
import jax.numpy as jnp
from jax import lax
from jax.sharding import PartitionSpec as P


def lower_half(matrix):
    return jnp.tril(matrix, -1) + 0.5 * jnp.diag(jnp.diag(matrix))


def product(left_side, right_side):
    return jnp.dot(
        left_side, right_side, precision=lax.Precision.HIGHEST, preferred_element_type=jnp.float32
    )


def right_solve(factor, row_block):
    return jax.scipy.linalg.solve_triangular(factor, row_block.T, trans=1, lower=True).T


def diag_adjoint(factor, adjoint):
    inner_term = lower_half(product(factor.T, adjoint))
    halfway = jax.scipy.linalg.solve_triangular(factor, inner_term, trans=1, lower=True)
    whole_term = right_solve(factor, halfway)
    return 0.5 * (whole_term + whole_term.T)


def shards(
    factor_diag, factor_mid, factor_low, adjoint_diag, adjoint_mid, adjoint_low, trailing_adjoint
):
    block_rows, row_groups, group_cols = trailing_adjoint.shape
    local_block = trailing_adjoint.reshape(block_rows, row_groups * group_cols)

    def image_of(panel):
        columns = lax.all_gather(panel, "row", axis=0, tiled=True)
        return lax.psum_scatter(
            product(local_block, columns), "col", scatter_dimension=0, tiled=True
        )

    second_image = image_of(factor_low[1])
    first_image = image_of(factor_low[0])
    second_solved = right_solve(factor_diag[1], adjoint_low[1] - 2.0 * second_image)
    second_total = lax.psum(product(second_solved.T, factor_low[1]), ("row", "col"))
    second_grad = diag_adjoint(factor_diag[1], adjoint_diag[1] - second_total)
    second_half = 0.5 * second_solved
    upper_term = product(second_half.T, factor_low[0])
    bottom_rows = adjoint_low[0] - 2.0 * (product(second_half, factor_mid) + first_image)
    bottom_solved = right_solve(factor_diag[0], bottom_rows)
    lower_term = product(bottom_solved.T, factor_low[0])
    upper_total = lax.psum(upper_term, ("row", "col"))
    lower_total = lax.psum(lower_term, ("row", "col"))
    top_rows = adjoint_mid - 2.0 * (product(second_grad, factor_mid) + upper_total)
    top_solved = right_solve(factor_diag[0], top_rows)
    first_adjoint = adjoint_diag[0] - product(top_solved.T, factor_mid) - lower_total
    first_grad = diag_adjoint(factor_diag[0], first_adjoint)
    return (
        jnp.stack([first_grad, second_grad]),
        0.5 * top_solved,
        jnp.stack([0.5 * bottom_solved, second_half]),
    )


def solution(mesh):
    return jax.shard_map(
        shards,
        mesh=mesh,
        in_specs=(
            P(),
            P(),
            P(None, ("row", "col"), None),
            P(),
            P(),
            P(None, ("row", "col"), None),
            P("row", None, "col"),
        ),
        out_specs=(P(), P(), P(None, ("row", "col"), None)),
        check_vma=False,
    )
```

profile of v0, /device:TPU:2, one launch (start us, length us, event | category | flops | bytes accessed | tf_op | source)
XLA Modules:
  0.0 587.7 jit_solution(3043104510383694873)
XLA Ops:
  7.2 1.8 fusion.165
  9.1 0.7 all-gather.7.cloned.1.call-update
  9.8 53.8 %all-gather.5.cloned.1.call-done = f32[1,1024,512]{2,1,0:T(8,128)} async-done(((f32[1,64,512]{2,1,0:T(8,128)}), f32[1,1024,512]{2,1,0:T(8,128)}) %all-gather.5.cloned.1.call-update) | async-done | bytes 2097168 | tf_op jit(solution)/shard_map/all_gather | solution.py:35
  63.6 10.2 %fusion.2 = f32[1024,512]{1,0:T(8,128)} fusion(f32[1024,1024]{0,1:T(8,128)} %bitcast.202, f32[1,1024,512]{2,1,0:T(8,128)} %all-gather.5.cloned.1.call-done), kind=kOutput, calls=%fused_computation.9 | convolution fusion | flops 6442450944 | bytes 8388608 | tf_op jit(solution)/shard_map/dot_general | solution.py:12
  73.8 1.5 copy-done.1
  75.3 1.6 bitcast_select_fusion.1
  76.9 39.0 %all-gather.7.cloned.1.call-done = f32[1,1024,512]{2,1,0:T(8,128)} async-done(((f32[1,64,512]{2,1,0:T(8,128)}), f32[1,1024,512]{2,1,0:T(8,128)}) %all-gather.7.cloned.1.call-update) | async-done | bytes 2097168 | tf_op jit(solution)/shard_map/all_gather | solution.py:35
  115.9 10.2 %fusion = f32[1024,512]{1,0:T(8,128)} fusion(f32[1024,1024]{0,1:T(8,128)} %bitcast.203, f32[1,1024,512]{2,1,0:T(8,128)} %all-gather.7.cloned.1.call-done), kind=kOutput, calls=%fused_computation.7 | convolution fusion | flops 6442450944 | bytes 8388608 | tf_op jit(solution)/shard_map/dot_general | solution.py:12
  126.4 12.0 %while.14 = (s32[]{:T(128)}, f32[512,512]{1,0:T(8,128)}, s32[4,2]{0,1:T(2,128)S(1)}, f32[4,128,128]{2,1,0:T(8,128)S(1)}, s32[]{:T(128)}) while((s32[]{:T(128)}, f32[512,512]{1,0:T(8,128)}, s32[4,2]{0,1:T(2,128)S(1)}, f32[4,128,128]{2,1,0:T(8,128)S(1)}, s32[]{:T(128)}) %tuple.62), condition=%wide.while_cond.1.clone, body=%wide.while_body.1.clone.sunk | while | flops 2 | bytes 131181 | solution.py:18
  127.1 2.3 bitcast_dynamic-update-slice_fusion.4
  130.1 2.3 bitcast_dynamic-update-slice_fusion.4
  133.1 2.3 bitcast_dynamic-update-slice_fusion.4
  136.2 2.3 bitcast_dynamic-update-slice_fusion.4
  138.5 39.3 %custom-call.17 = f32[4,128,128]{1,2,0:T(8,128)S(1)} custom-call(f32[4,128,128]{2,1,0:T(8,128)S(1)} %get-tuple-element.53), custom_call_target="InvertDiagBlocksLowerTriangular" | custom-call | tf_op jit(solution)/shard_map/jit(_solve_triangular)/triangular_solve | solution.py:18
  177.8 7.7 %while.15 = (s32[]{:T(128)}, f32[512,512]{1,0:T(8,128)S(1)}, s32[4,2]{0,1:T(2,128)S(1)}, f32[4,128,128]{2,1,0:T(8,128)S(1)}, s32[]{:T(128)}) while((s32[]{:T(128)}, f32[512,512]{1,0:T(8,128)S(1)}, s32[4,2]{0,1:T(2,128)S(1)}, f32[4,128,128]{2,1,0:T(8,128)S(1)}, s32[]{:T(128)}) %tuple.80), condition=%wide.while_cond.1.clone.3, body=%wide.while_body.1.clone.3.sunk | while | flops 2 | bytes 131181 | solution.py:18
  178.4 1.3 bitcast_dynamic-update-slice_fusion.5
  180.4 1.3 bitcast_dynamic-update-slice_fusion.5
  182.3 1.3 bitcast_dynamic-update-slice_fusion.5
  184.2 1.3 bitcast_dynamic-update-slice_fusion.5
  185.5 0.7 copy-done.21
  186.2 40.1 %custom-call.21 = f32[4,128,128]{1,2,0:T(8,128)S(1)} custom-call(f32[4,128,128]{2,1,0:T(8,128)} %copy-done.21), custom_call_target="InvertDiagBlocksLowerTriangular" | custom-call | tf_op jit(solution)/shard_map/jit(_solve_triangular)/triangular_solve | solution.py:18
  226.4 1.0 fusion.81
  227.6 1.0 convolution_subtract_fusion.21
  228.9 1.1 convolution_subtract_fusion.20
  230.3 1.2 convolution_subtract_fusion.19
  231.7 2.0 fusion.77
  233.8 2.0 fusion.79
  235.8 5.0 reduce-scatter.5.cloned.1.call-done
  240.7 1.7 fusion.10
  244.1 2.0 fusion.75
  246.3 0.7 pad_maximum_fusion.5
  247.0 265.8 %all-reduce.3.cloned.1.call-done = (f32[512,512]{1,0:T(8,128)}, f32[512,512]{1,0:T(8,128)}, f32[512,512]{1,0:T(8,128)}) async-done(((f32[512,512]{1,0:T(8,128)}, f32[512,512]{1,0:T(8,128)}, f32[512,512]{1,0:T(8,128)}), (f32[512,512]{1,0:T(8,128)}, f32[512,512]{1,0:T(8,128)}, f32[512,512]{1,0:T(8,128)})) %all-reduce.3.cloned.1.call-update) | async-done | bytes 3145744 | tf_op jit(solution)/shard_map/psum | solution.py:43
  512.8 3.7 convolution_bitcast_fusion.1
  516.5 4.8 gather_fusion
  523.5 1.0 convolution_subtract_fusion.9
  524.9 1.5 convolution_subtract_fusion.15
  528.2 1.0 convolution_subtract_fusion.7
  529.6 1.5 convolution_subtract_fusion.14
  531.5 1.3 fusion.111
  532.8 0.7 copy-done.13
  533.5 1.0 fusion.42
  534.6 1.6 copy.29
  536.2 3.8 fusion.7
  540.4 1.0 convolution_subtract_fusion.6
  541.8 1.0 convolution_subtract_fusion.5
  543.9 2.2 convolution_subtract_fusion.13
  546.1 1.1 copy.31
  547.1 1.1 copy.32
  548.4 1.5 fusion.123
  549.9 1.0 multiply_bitcast_fusion
  550.9 3.4 fusion.4
  554.3 1.9 convolution_bitcast_fusion
  556.2 4.7 gather_fusion.1
  563.2 1.0 convolution_subtract_fusion.3
  564.6 1.5 convolution_subtract_fusion.12
  567.9 1.0 convolution_subtract_fusion.1
  569.3 1.5 convolution_subtract_fusion.11
  570.8 0.8 copy.35
  571.6 0.8 copy.36
  572.4 0.8 copy.37
  574.4 1.2 fusion.41
  575.6 1.3 copy.38
  576.9 2.1 multiply_bitcast_fusion.1
  579.2 1.8 copy.39
  (116 shorter events, 21.2 us)
Async XLA Ops:
  7.2 233.6 %copy-start = (f32[512,512]{1,0:T(8,128)S(1)}, f32[512,512]{1,0:T(8,128)}, u32[]{:S(2)}) copy-start(f32[512,512]{1,0:T(8,128)} %param.12) | copy-start | bytes 3145732
  7.2 56.4 %all-gather.5.cloned.1.call-start = ((), (), s32[]{:S(2)}) async-start(), calls=%async_computation.4 | async-start | bytes 2228224 | tf_op jit(solution)/shard_map/all_gather | solution.py:35
  9.0 106.9 %all-gather.7.cloned.1.call-start = ((), (), s32[]{:S(2)}) async-start(), calls=%async_computation.5 | async-start | bytes 2228224 | tf_op jit(solution)/shard_map/all_gather | solution.py:35
  9.8 216.6 %reduce-scatter.3.cloned.1.call-start = ((), (), s32[]{:S(2)}) async-start(), calls=%async_computation.2 | async-start | bytes 2228224 | tf_op jit(solution)/shard_map/reduce_scatter | solution.py:36
  73.8 1.6 copy-start.1
  73.8 166.9 %reduce-scatter.5.cloned.1.call-start = ((), (), s32[]{:S(2)}) async-start(), calls=%async_computation.3 | async-start | bytes 2228224 | tf_op jit(solution)/shard_map/reduce_scatter | solution.py:36
  126.1 51.7 %copy-start.3 = (f32[512,512]{1,0:T(8,128)S(1)}, f32[512,512]{1,0:T(8,128)}, u32[]{:S(2)}) copy-start(f32[512,512]{1,0:T(8,128)} %get-tuple-element.169) | copy-start | bytes 3145732
  126.1 100.3 %copy-start.20 = (f32[2,64,512]{2,1,0:T(8,128)S(1)}, f32[2,64,512]{2,1,0:T(8,128)}, u32[]{:S(2)}) copy-start(f32[2,64,512]{2,1,0:T(8,128)} %param.16) | copy-start | bytes 786436
  126.1 105.6 %copy-start.19 = (f32[2,64,512]{2,1,0:T(8,128)S(1)}, f32[2,64,512]{2,1,0:T(8,128)}, u32[]{:S(2)}) copy-start(f32[2,64,512]{2,1,0:T(8,128)} %param.13) | copy-start | bytes 786436
  126.2 386.6 %all-reduce.3.cloned.1.call-start = ((), (), s32[]{:S(2)}) async-start(), calls=%async_computation.6 | async-start | bytes 6291456 | tf_op jit(solution)/shard_map/psum | solution.py:43
  177.8 351.5 %copy-start.15 = (f32[4,128,128]{1,2,0:T(8,128)}, f32[4,128,128]{1,2,0:T(8,128)S(1)}, u32[]{:S(2)}) copy-start(f32[4,128,128]{1,2,0:T(8,128)S(1)} %custom-call.17) | copy-start | bytes 786436
  185.5 0.7 copy-start.21
  226.3 19.8 %copy-start.6 = (f32[4,128,128]{1,2,0:T(8,128)}, f32[4,128,128]{1,2,0:T(8,128)S(1)}, u32[]{:S(2)}) copy-start(f32[4,128,128]{1,2,0:T(8,128)S(1)} %custom-call.21) | copy-start | bytes 786436
  521.3 1.2 copy-start.5
  531.2 4.9 copy-start.9
  531.4 1.4 copy-start.11
  531.5 1.3 copy-start.12
  532.8 0.7 copy-start.13
  536.2 3.8 copy-start.7
  541.8 1.4 copy-start.14
  543.2 0.7 copy-start.16
  548.4 2.6 copy-start.18
  550.9 3.4 copy-start.2
  556.2 4.9 copy-start.8
  561.0 1.2 copy-start.4
  573.7 0.7 copy-start.17
  574.4 2.5 copy-start.10
Sparse Core Ops, SparseCore 0:
  11.0 52.5 all-gather.4
  66.6 49.3 all-gather.6
  119.0 60.2 reduce-scatter.2
  181.7 58.9 reduce-scatter.4
  246.9 265.8 all-reduce.2
where the time goes:
time: 594 us; the launch traced here: 588 us
  waiting for transfers between devices  364 us (61%)
  other arithmetic  88.8 us (15%)
  matrix products  72.9 us (12%)
  local copies, waits for them, and re-layouts  46.4 us (8%)
  between operations  14.8 us (2%)
    psum x1, waiting for transfers between devices, shards(): lax.psum(product(second_solved.T, factor_low[1]), ('row', 'col'))  266 us
    all_gather x2, waiting for transfers between devices, image_of(): columns = lax.all_gather(panel, 'row', axis=0, tiled=True)  92.8 us
    another operation x4, other arithmetic, right_solve(): jax.scipy.linalg.solve_triangular(factor, row_block.T, trans=1, lower=True)  81 us
    dot_general x10, matrix products, product(): jnp.dot(left_side, right_side, precision=lax.Precision.HIGHEST, preferred...  41 us
    another operation x36, local copies, waits for them, and re-layouts, right_solve(): jax.scipy.linalg.solve_triangular(factor, row_block.T, trans=1, lower=True)  24.7 us
    another operation x35, matrix products, right_solve(): jax.scipy.linalg.solve_triangular(factor, row_block.T, trans=1, lower=True)  22.8 us
  transfers between devices with their start and end apart: 5, of which 4 were waited for; matrix products, arithmetic and copies ran while one was open for 22% of the time, Pallas kernels for 0%

commit v1 on v0

--- a/solution.py
+++ b/solution.py
@@ -32,7 +32,9 @@
     local_block = trailing_adjoint.reshape(block_rows, row_groups * group_cols)
 
     def image_of(panel):
-        columns = lax.all_gather(panel, "row", axis=0, tiled=True)
+        columns = jnp.concatenate(
+            lax.all_to_all(jnp.stack([panel] * lax.axis_size("row")), "row", 0, 0), axis=0
+        )
         return lax.psum_scatter(
             product(local_block, columns), "col", scatter_dimension=0, tiled=True
         )

time: 594 us -> 564 us (0.949)
  waiting for transfers between devices: 364 us -> 293 us
  blocking collectives: 0 us -> 34.6 us
    all_gather x2 -> x0, waiting for transfers between devices: 92.8 us -> none  [image_of(): columns = lax.all_gather(panel, 'row', axis=0, tiled=True)]
    all_to_all x0 -> x1, blocking collectives: none -> 34.6 us  [image_of(): lax.all_to_all(jnp.stack([panel] * lax.axis_size('row')), 'row', 0, 0)]
    all_to_all x0 -> x1, waiting for transfers between devices: none -> 24.6 us  [image_of(): lax.all_to_all(jnp.stack([panel] * lax.axis_size('row')), 'row', 0, 0)]
  transfers between devices with their start and end apart: 5 -> 4, of which waited for: 4 -> 2; matrix products, arithmetic and copies ran while one was open for 22% -> 22% of each run, Pallas kernels for 0% -> 0%
where the time goes in v1:
time: 564 us; the launch traced here: 555 us
  waiting for transfers between devices  293 us (52%)
  other arithmetic  88.8 us (16%)
  matrix products  70.8 us (13%)
  local copies, waits for them, and re-layouts  46.5 us (8%)
  blocking collectives  34.6 us (6%)
  between operations  14.8 us (3%)
  starting transfers between devices  6.04 us (1%)
    psum x1, waiting for transfers between devices, shards(): lax.psum(product(second_solved.T, factor_low[1]), ('row', 'col'))  268 us
    another operation x4, other arithmetic, right_solve(): jax.scipy.linalg.solve_triangular(factor, row_block.T, trans=1, lower=True)  81 us
    dot_general x10, matrix products, product(): jnp.dot(left_side, right_side, precision=lax.Precision.HIGHEST, preferred...  38.9 us
    all_to_all x1, blocking collectives, image_of(): lax.all_to_all(jnp.stack([panel] * lax.axis_size('row')), 'row', 0, 0)  34.6 us
    another operation x36, local copies, waits for them, and re-layouts, right_solve(): jax.scipy.linalg.solve_triangular(factor, row_block.T, trans=1, lower=True)  25.2 us
    all_to_all x1, waiting for transfers between devices, image_of(): lax.all_to_all(jnp.stack([panel] * lax.axis_size('row')), 'row', 0, 0)  24.6 us
    another operation x35, matrix products, right_solve(): jax.scipy.linalg.solve_triangular(factor, row_block.T, trans=1, lower=True)  22.8 us
  transfers between devices with their start and end apart: 4, of which 2 were waited for; matrix products, arithmetic and copies ran while one was open for 22% of the time, Pallas kernels for 0%

profile of v1, /device:TPU:2, one launch (start us, length us, event | category | flops | bytes accessed | tf_op | source)
XLA Modules:
  0.0 554.6 jit_solution(13381320104166079622)
XLA Ops:
  7.2 1.1 slice_bitcast_fusion
  8.6 34.6 %all_to_all.10 = f32[16,64,512]{2,1,0:T(8,128)S(1)} all-to-all(f32[16,64,512]{2,1,0:T(8,128)S(1)} %stack.24), channel_id=1, replica_groups=mesh['row'=16,'col'=16] {'row'}, dimensions={0} | all-to-all | bytes 4194304 | tf_op jit(solution)/shard_map/all_to_all | solution.py:36
  43.1 8.1 %convolution_bitcast_fusion.1 = f32[1024,512]{1,0:T(8,128)} fusion(f32[1024,16,64]{0,2,1:T(8,128)S(1)} %copy-done.22, f32[16,64,512]{2,1,0:T(8,128)S(1)} %all_to_all.10), kind=kOutput, calls=%fused_computation.8 | convolution fusion | flops 6442450944 | bytes 8388608 | tf_op jit(solution)/shard_map/dot_general | solution.py:12
  51.2 1.6 stack.25
  52.8 5.7 %all-to-all-start.1 = ((f32[16,64,512]{2,1,0:T(8,128)}), f32[16,64,512]{2,1,0:T(8,128)}, u32[]{:S(2)}, u32[]{:S(2)}) async-start(f32[16,64,512]{2,1,0:T(8,128)} %stack.25), calls=%async_computation.2 | async-start | bytes 4194304 | tf_op jit(solution)/shard_map/all_to_all | solution.py:36
  58.7 1.6 bitcast_select_fusion.1
  60.2 24.6 %all-to-all-done.1 = f32[16,64,512]{2,1,0:T(8,128)} async-done(((f32[16,64,512]{2,1,0:T(8,128)}), f32[16,64,512]{2,1,0:T(8,128)}, u32[]{:S(2)}, u32[]{:S(2)}) %all-to-all-start.1) | async-done | bytes 2097184 | tf_op jit(solution)/shard_map/all_to_all | solution.py:36
  84.8 10.2 %convolution_bitcast_fusion = f32[1024,512]{1,0:T(8,128)} fusion(f32[1024,16,64]{0,2,1:T(8,128)} %param.17, f32[16,64,512]{2,1,0:T(8,128)} %all-to-all-done.1), kind=kOutput, calls=%fused_computation.7 | convolution fusion | flops 6442450944 | bytes 8388608 | tf_op jit(solution)/shard_map/dot_general | solution.py:12
  95.3 12.2 %while.14 = (s32[]{:T(128)}, f32[512,512]{1,0:T(8,128)}, s32[4,2]{0,1:T(2,128)S(1)}, f32[4,128,128]{2,1,0:T(8,128)S(1)}, s32[]{:T(128)}) while((s32[]{:T(128)}, f32[512,512]{1,0:T(8,128)}, s32[4,2]{0,1:T(2,128)S(1)}, f32[4,128,128]{2,1,0:T(8,128)S(1)}, s32[]{:T(128)}) %tuple.62), condition=%wide.while_cond.1.clone, body=%wide.while_body.1.clone.sunk | while | flops 2 | bytes 131181 | solution.py:18
  96.0 2.4 bitcast_dynamic-update-slice_fusion.4
  99.0 2.4 bitcast_dynamic-update-slice_fusion.4
  102.1 2.4 bitcast_dynamic-update-slice_fusion.4
  105.2 2.3 bitcast_dynamic-update-slice_fusion.4
  107.5 39.3 %custom-call.17 = f32[4,128,128]{1,2,0:T(8,128)S(1)} custom-call(f32[4,128,128]{2,1,0:T(8,128)S(1)} %get-tuple-element.53), custom_call_target="InvertDiagBlocksLowerTriangular" | custom-call | tf_op jit(solution)/shard_map/jit(_solve_triangular)/triangular_solve | solution.py:18
  146.9 7.9 %while.15 = (s32[]{:T(128)}, f32[512,512]{1,0:T(8,128)S(1)}, s32[4,2]{0,1:T(2,128)S(1)}, f32[4,128,128]{2,1,0:T(8,128)S(1)}, s32[]{:T(128)}) while((s32[]{:T(128)}, f32[512,512]{1,0:T(8,128)S(1)}, s32[4,2]{0,1:T(2,128)S(1)}, f32[4,128,128]{2,1,0:T(8,128)S(1)}, s32[]{:T(128)}) %tuple.76), condition=%wide.while_cond.1.clone.3, body=%wide.while_body.1.clone.3.sunk | while | flops 2 | bytes 131181 | solution.py:18
  147.5 1.3 bitcast_dynamic-update-slice_fusion.5
  149.5 1.3 bitcast_dynamic-update-slice_fusion.5
  151.5 1.3 bitcast_dynamic-update-slice_fusion.5
  153.5 1.3 bitcast_dynamic-update-slice_fusion.5
  154.9 0.7 copy-done.21
  155.6 40.1 %custom-call.21 = f32[4,128,128]{1,2,0:T(8,128)S(1)} custom-call(f32[4,128,128]{2,1,0:T(8,128)} %copy-done.21), custom_call_target="InvertDiagBlocksLowerTriangular" | custom-call | tf_op jit(solution)/shard_map/jit(_solve_triangular)/triangular_solve | solution.py:18
  195.7 1.0 fusion.71
  197.0 1.0 convolution_subtract_fusion.21
  198.3 1.1 convolution_subtract_fusion.20
  199.6 1.2 convolution_subtract_fusion.19
  201.1 2.0 fusion.76
  203.1 2.0 fusion.151
  205.1 1.7 fusion.6
  208.5 2.0 fusion.92
  210.7 0.7 pad_maximum_fusion.5
  211.4 268.3 %all-reduce.3.cloned.1.call-done = (f32[512,512]{1,0:T(8,128)}, f32[512,512]{1,0:T(8,128)}, f32[512,512]{1,0:T(8,128)}) async-done(((f32[512,512]{1,0:T(8,128)}, f32[512,512]{1,0:T(8,128)}, f32[512,512]{1,0:T(8,128)}), (f32[512,512]{1,0:T(8,128)}, f32[512,512]{1,0:T(8,128)}, f32[512,512]{1,0:T(8,128)})) %all-reduce.3.cloned.1.call-update) | async-done | bytes 3145744 | tf_op jit(solution)/shard_map/psum | solution.py:45
  479.7 3.7 convolution_bitcast_fusion.3
  483.4 4.8 gather_fusion
  490.4 1.0 convolution_subtract_fusion.9
  491.8 1.5 convolution_subtract_fusion.15
  495.1 1.0 convolution_subtract_fusion.7
  496.5 1.5 convolution_subtract_fusion.14
  498.4 1.3 fusion.103
  499.7 0.7 copy-done.13
  500.4 1.0 fusion.38
  501.5 1.6 copy.29
  503.0 3.8 fusion.3
  507.3 1.0 convolution_subtract_fusion.6
  508.7 1.0 convolution_subtract_fusion.5
  510.8 2.2 convolution_subtract_fusion.13
  512.9 1.1 copy.31
  514.0 1.1 copy.32
  515.3 1.5 fusion.115
  516.8 1.0 multiply_bitcast_fusion
  517.8 3.4 fusion
  521.2 1.9 convolution_bitcast_fusion.2
  523.1 4.7 gather_fusion.1
  530.1 1.0 convolution_subtract_fusion.3
  531.4 1.5 convolution_subtract_fusion.12
  534.8 1.0 convolution_subtract_fusion.1
  536.2 1.5 convolution_subtract_fusion.11
  537.7 0.8 copy.35
  538.5 0.8 copy.36
  539.3 0.8 copy.37
  540.5 0.7 copy-done.17
  541.2 1.2 fusion.37
  542.5 1.3 copy.38
  543.8 2.1 multiply_bitcast_fusion.1
  546.1 1.8 copy.39
  (117 shorter events, 20.8 us)
Async XLA Ops:
  7.2 198.0 %copy-start = (f32[512,512]{1,0:T(8,128)S(1)}, f32[512,512]{1,0:T(8,128)}, u32[]{:S(2)}) copy-start(f32[512,512]{1,0:T(8,128)} %param.12) | copy-start | bytes 3145732
  7.2 188.5 %reduce-scatter.3.cloned.1.call-start = ((), (), s32[]{:S(2)}) async-start(), calls=%async_computation.4 | async-start | bytes 2228224 | tf_op jit(solution)/shard_map/reduce_scatter | solution.py:38
  8.6 34.6 %copy-start.22 = (f32[1024,16,64]{0,2,1:T(8,128)S(1)}, f32[1024,16,64]{0,2,1:T(8,128)}, u32[]{:S(2)}) copy-start(f32[1024,16,64]{0,2,1:T(8,128)} %param.17) | copy-start | bytes 12582916
  52.8 5.8 %copy-start.1 = (f32[2,512,512]{2,1,0:T(8,128)S(1)}, f32[2,512,512]{2,1,0:T(8,128)}, u32[]{:S(2)}) copy-start(f32[2,512,512]{2,1,0:T(8,128)} %param.11) | copy-start | bytes 6291460
  52.8 32.0 %all-to-all-start.1 = ((f32[16,64,512]{2,1,0:T(8,128)}), f32[16,64,512]{2,1,0:T(8,128)}, u32[]{:S(2)}, u32[]{:S(2)}) async-start(f32[16,64,512]{2,1,0:T(8,128)} %stack.25), calls=%async_computation.2 | async-start | bytes 4194304 | tf_op jit(solution)/shard_map/all_to_all | solution.py:36
  58.6 146.5 %reduce-scatter.5.cloned.1.call-start = ((), (), s32[]{:S(2)}) async-start(), calls=%async_computation.5 | async-start | bytes 2228224 | tf_op jit(solution)/shard_map/reduce_scatter | solution.py:38
  95.0 51.9 %copy-start.3 = (f32[512,512]{1,0:T(8,128)S(1)}, f32[512,512]{1,0:T(8,128)}, u32[]{:S(2)}) copy-start(f32[512,512]{1,0:T(8,128)} %get-tuple-element.169) | copy-start | bytes 3145732
  95.0 100.7 %copy-start.20 = (f32[2,64,512]{2,1,0:T(8,128)S(1)}, f32[2,64,512]{2,1,0:T(8,128)}, u32[]{:S(2)}) copy-start(f32[2,64,512]{2,1,0:T(8,128)} %param.16) | copy-start | bytes 786436
  95.0 106.1 %copy-start.19 = (f32[2,64,512]{2,1,0:T(8,128)S(1)}, f32[2,64,512]{2,1,0:T(8,128)}, u32[]{:S(2)}) copy-start(f32[2,64,512]{2,1,0:T(8,128)} %param.13) | copy-start | bytes 786436
  95.0 384.7 %all-reduce.3.cloned.1.call-start = ((), (), s32[]{:S(2)}) async-start(), calls=%async_computation.6 | async-start | bytes 6291456 | tf_op jit(solution)/shard_map/psum | solution.py:45
  146.8 349.3 %copy-start.15 = (f32[4,128,128]{1,2,0:T(8,128)}, f32[4,128,128]{1,2,0:T(8,128)S(1)}, u32[]{:S(2)}) copy-start(f32[4,128,128]{1,2,0:T(8,128)S(1)} %custom-call.17) | copy-start | bytes 786436
  154.8 0.7 copy-start.21
  195.7 14.9 %copy-start.6 = (f32[4,128,128]{1,2,0:T(8,128)}, f32[4,128,128]{1,2,0:T(8,128)S(1)}, u32[]{:S(2)}) copy-start(f32[4,128,128]{1,2,0:T(8,128)S(1)} %custom-call.21) | copy-start | bytes 786436
  488.2 1.2 copy-start.5
  498.1 4.9 copy-start.9
  498.3 1.4 copy-start.11
  498.4 1.3 copy-start.12
  499.7 0.7 copy-start.13
  503.0 3.8 copy-start.7
  508.6 1.4 copy-start.14
  510.1 0.7 copy-start.16
  515.2 2.6 copy-start.18
  517.8 3.4 copy-start.2
  523.1 4.9 copy-start.8
  527.9 1.2 copy-start.4
  540.5 0.7 copy-start.17
  541.2 2.5 copy-start.10
Sparse Core Ops, SparseCore 0:
  51.4 60.9 reduce-scatter.2
  114.8 59.0 reduce-scatter.4
  210.7 268.9 all-reduce.2
